TPU v7x, 32 devices: a whole 2x2x4 slice. The times are simulated.
32 devices in a mesh: echo: 2 (over x), coil: 8 (over z, core), read: 2 (over y).
Axes of the slice: x: 2, y: 2, z: 4, core: 2. Of those that a mesh axis runs over, the one named last changes fastest.
Arguments:
- kspace: bfloat16 [384, 2, 8, 4, 2, 192], P(None, 'echo', 'coil', 'read'), may hold values from -3 to 3
- sampling: int32 [384, 2, 192], P(None, 'echo'), may hold values 0 or 1
- coil_maps: bfloat16 [384, 8, 4, 2, 192], P(None, 'coil', 'read'), may hold values from -1.5 to 1.5
- image: float32 [384, 2, 4, 2, 192], P('coil', 'echo', 'read'), may hold values from -6 to 6
- filters: bfloat16 [48, 3, 3, 3, 2], replicated, may hold values from -0.875 to 0.875
- thresholds: float32 [48], replicated, may hold values from 0.5 to 8
- dc_weight: float32 [2], P('echo'), may hold values from 0.5 to 2
Outputs:
- updated: float32 [384, 2, 4, 2, 192], P('coil', 'echo', 'read')
All inputs are finite; a program needn't handle non-finite values. No bound on the sum of `sampling` on one device may be relied on, other than what follows from the above.
Results may differ from a plain program's by a relative error of at most 0.0033.
Values may be sent and summed in bfloat16 or wider, within the bound.
A program may use at most 128 MiB of HBM per device.

v0:
```python
import functools

import numpy as np
import jax
import jax.numpy as jnp
from jax import lax
from jax.experimental import pallas as pl
from jax.experimental.pallas import tpu as pltpu
from jax.sharding import PartitionSpec as P

MESH = pl.DeviceIdType.MESH
F32 = jnp.float32
BF16 = jnp.bfloat16
SLAB = 32
GRANT = 24 << 20


def tables(length):
    product = np.outer(np.arange(length), np.arange(length)) % length
    phases = product * (2.0 * np.pi / length)
    normalize = length ** (-0.5)
    return np.cos(phases) * normalize, np.sin(phases) * normalize


def window_rows(rows, peers):
    for size in range(2, rows + 1):
        if rows % size == 0 and rows // size <= peers:
            return size
    return rows


def dot(left, right):
    return jnp.dot(left, right, preferred_element_type=F32)


def kernel(
    cfg,
    dc_ref, img_ref, xs_ref, kspace_hbm, maps_hbm, samp_hbm, fz_hbm, az_hbm, ty_hbm,
    filters_ref, spread_hbm, thr_ref,
    adj_ref, pen_ref,
    gat, part, paired, rs_send, rs_recv, wide_ref, tall_ref, level, ext, edge, pen_send, pen_recv, pacc, slab,
    kspace, maps, samp, fz, az, ty, spread,
    local_sem, ag_send_sem, ag_recv_sem, x_send_sem, x_recv_sem, e_send_sem, e_recv_sem,
    p_send_sem, p_recv_sem, rs_send_sem, rs_recv_sem, f_send_sem, f_recv_sem, pair_send_sem, pair_recv_sem,
):
    n_e, n_c, n_r, n_q, rq, nz, ny = cfg
    peers = n_e * n_r
    e = lax.axis_index("echo")
    c = lax.axis_index("coil")
    r = lax.axis_index("read")
    q = e * n_r + r
    s_local, rb = rs_send.shape[0], img_ref.shape[0]
    chips = n_c // 2
    core = lax.rem(c, 2)
    chip = c // 2
    partner = c + 1 - 2 * core
    width = 2 * nz
    zp = ext.shape[-1]

    loads = [
        pltpu.make_async_copy(src, dst, local_sem.at[i])
        for i, (src, dst) in enumerate(
            [(spread_hbm, spread), (kspace_hbm, kspace), (maps_hbm, maps), (samp_hbm, samp), (fz_hbm, fz), (az_hbm, az), (ty_hbm, ty)]
        )
    ]

    for load in loads:
        load.start()

    def remote(src, dst, send, recv, target):
        return pltpu.make_async_remote_copy(
            src_ref=src, dst_ref=dst, send_sem=send, recv_sem=recv, device_id=target, device_id_type=MESH
        )

    def when(condition, act):
        if condition is True:
            act()
        else:
            pl.when(condition)(act)

    def up(d):
        return lax.rem(q + d, peers)

    def down(d):
        return lax.rem(q + peers - d, peers)

    def active(which):
        return True if n_q == peers else which < n_q

    barrier = pltpu.get_barrier_semaphore()
    for d in range(chips):
        to = lax.rem(c + 2 * d, n_c) if d else partner
        pl.semaphore_signal(barrier, inc=1, device_id=(e, to, r), device_id_type=MESH)
    for d in range(peers):
        if d:
            pl.semaphore_signal(barrier, inc=1, device_id=(up(d) // n_r, c, lax.rem(up(d), n_r)), device_id_type=MESH)
        for step, ok in ((1, c < n_c - 1), (-1, c > 0)):
            @pl.when(ok)
            def _():
                pl.semaphore_signal(
                    barrier, inc=1, device_id=(up(d) // n_r, c + step, lax.rem(up(d), n_r)), device_id_type=MESH
                )
    sides = jnp.minimum(c, 1) + jnp.minimum(n_c - 1 - c, 1)
    pl.semaphore_wait(barrier, chips + peers - 1 + peers * sides)

    def window(d):
        to = up(d)
        return remote(
            xs_ref.at[1 + to], ext.at[e, r], x_send_sem.at[d], x_recv_sem.at[d], (to // n_r, c, lax.rem(to, n_r))
        )

    last = n_q - 1
    edge_up = lambda: remote(
        xs_ref.at[n_q + 1], edge.at[e, r], e_send_sem.at[0], e_recv_sem.at[q], (0, c + 1, 0)
    )
    edge_down = lambda: remote(
        xs_ref.at[0], edge.at[e, r], e_send_sem.at[1], e_recv_sem.at[q], (last // n_r, c - 1, last % n_r)
    )
    for d in range(1, peers):
        when(active(up(d)), lambda: window(d).start())
    pl.when(c < n_c - 1)(lambda: edge_up().start())
    pl.when(c > 0)(lambda: edge_down().start())

    def gather(d):
        to = lax.rem(c + 2 * d, n_c) if d else partner
        return remote(img_ref, gat.at[c], ag_send_sem.at[d], ag_recv_sem.at[d], (e, to, r))

    def forward(d):
        src = lax.rem(c + n_c - 2 * d, n_c)
        return remote(gat.at[src], gat.at[src], f_send_sem.at[d], f_recv_sem.at[d], (e, partner, r))

    for d in range(chips):
        gather(d).start()
    gat[c] = img_ref[...]

    count = filters_ref.shape[-1]
    slices = s_local * n_r
    flat_filters = filters_ref[...].astype(F32).reshape(-1, count).astype(BF16)
    loads[0].wait()
    pieces = [dot(spread[at], flat_filters) for at in range(slices)]
    for at in range(slices):
        wide_ref[:, at * count : (at + 1) * count] = pieces[at].astype(BF16)
        tall_ref[at * count : (at + 1) * count, :] = pieces[at].T.astype(BF16)
    shape = (slices, count, count)
    on = lax.broadcasted_iota(jnp.int32, shape, 1) == lax.broadcasted_iota(jnp.int32, shape, 2)
    column = jnp.sum(jnp.where(on, thr_ref[...].reshape(1, 1, count), 0.0), axis=2, keepdims=True)
    level[...] = jnp.broadcast_to(column, (slices, count, zp)).reshape(slices * count, zp)

    has_edge = jnp.logical_or(
        jnp.logical_and(q == 0, c > 0), jnp.logical_and(q == last, c < n_c - 1)
    )

    @pl.when(jnp.logical_not(has_edge))
    def _():
        edge[...] = jnp.zeros_like(edge)

    def prepare():
        ext[e, r] = xs_ref[1 + q]
        for d in range(1, peers):
            src = down(d)
            remote(
                xs_ref.at[0], ext.at[src // n_r, lax.rem(src, n_r)], x_send_sem.at[d], x_recv_sem.at[d], (e, c, r)
            ).wait_recv()

        @pl.when(has_edge)
        def _():
            for src in range(peers):
                remote(
                    xs_ref.at[0], edge.at[src // n_r, src % n_r], e_send_sem.at[0], e_recv_sem.at[src], (e, c, r)
                ).wait_recv()

        rows = rq + 4
        taps = 2 * s_local * n_r
        for echo in range(n_e):
            parts = [ext[echo, read].astype(F32) + edge[echo, read].astype(F32) for read in range(n_r)]
            block = jnp.concatenate(parts, axis=1) if n_r > 1 else parts[0]
            flat = block.reshape(rows * taps, zp)
            moved = [
                pltpu.roll(flat, 1, 1).reshape(rows, taps, zp),
                block,
                pltpu.roll(flat, zp - 1, 1).reshape(rows, taps, zp),
            ]
            fill = [jnp.zeros((rows, SLAB - 3 * taps, zp), F32)] if SLAB > 3 * taps else []
            slab[echo] = jnp.concatenate(moved + fill, axis=1).reshape(rows * SLAB, zp).astype(BF16)

        pacc[...] = jnp.zeros_like(pacc)

    def respond(begin, end):
        tall = tall_ref[...]
        wide = wide_ref[...]
        lane_ok = lax.broadcasted_iota(jnp.int32, (1, zp), 1) < nz
        first = c * rb + q * rq - 1

        def row(i, carry):
            start = pl.multiple_of(i * SLAB, SLAB)
            response = [dot(tall, slab[echo, pl.ds(start, 3 * SLAB), :]) for echo in range(n_e)]
            energy = response[0] * response[0]
            for other in response[1:]:
                energy = energy + other * other
            magnitude = jnp.sqrt(energy)
            factor = magnitude / (magnitude + level[...])
            inside = jnp.logical_and(first + i >= 0, first + i < ny)
            factor = jnp.where(jnp.logical_and(lane_ok, inside), factor, 0.0)
            for echo in range(n_e):
                spread = dot(wide, (response[echo] * factor).astype(BF16))
                for a in range(3):
                    pacc[echo, i + a] += spread[a * SLAB : (a + 1) * SLAB]
            return carry

        lax.fori_loop(begin, end, row, 0, unroll=True)

    def collect():
        taps = 2 * s_local * n_r
        for echo in range(n_e):
            held = pacc[echo, 2 : 2 + rq]
            low = pltpu.roll(held[:, :taps].reshape(rq * taps, zp), zp - 1, 1).reshape(rq, taps, zp)
            high = pltpu.roll(held[:, 2 * taps : 3 * taps].reshape(rq * taps, zp), 1, 1).reshape(rq, taps, zp)
            total = low + held[:, taps : 2 * taps] + high
            for read in range(n_r):
                pen_send[echo, read] = total[:, read * 2 * s_local : (read + 1) * 2 * s_local]
        pen_recv[q] = pen_send[e, r]

    def penalty_out(d):
        to = up(d)
        return remote(
            pen_send.at[to // n_r, lax.rem(to, n_r)], pen_recv.at[q], p_send_sem.at[d], p_recv_sem.at[d],
            (to // n_r, c, lax.rem(to, n_r)),
        )

    split = (rq + 2) * 2 // 3

    def before():
        prepare()
        respond(0, split)

    def after():
        respond(split, rq + 2)
        collect()
        for d in range(1, peers):
            penalty_out(d).start()

    when(active(q), before)

    for d in range(1, chips):
        src = lax.rem(c + n_c - 2 * d, n_c)
        remote(img_ref, gat.at[src], ag_send_sem.at[d], ag_recv_sem.at[d], (e, partner, r)).wait_recv()
        forward(d).start()
    remote(img_ref, gat.at[partner], ag_send_sem.at[0], ag_recv_sem.at[0], (e, partner, r)).wait_recv()
    for d in range(1, chips):
        src = lax.rem(partner + n_c - 2 * d, n_c)
        remote(gat.at[src], gat.at[src], f_send_sem.at[d], f_recv_sem.at[d], (e, partner, r)).wait_recv()
    for load in loads[1:]:
        load.wait()

    def pair(s):
        return remote(
            part.at[s, :, 1 - core], paired.at[s], pair_send_sem.at[s], pair_recv_sem.at[s], (e, partner, r)
        )

    def scatter(s, d):
        to = lax.rem(chip + d, chips)
        return remote(
            rs_send.at[s, to], rs_recv.at[s, chip], rs_send_sem.at[s, d], rs_recv_sem.at[s, d],
            (e, 2 * to + core, r),
        )

    def send_sums(s):
        pair(s).wait_recv()
        rs_send[s] = (part[s, :, core].astype(F32) + paired[s].astype(F32)).astype(BF16)
        for d in range(1, chips):
            scatter(s, d).start()

    sampled = samp[...].astype(F32)
    for s in range(s_local):
        image = gat[:, :, s * width : (s + 1) * width].astype(F32).reshape(ny, width).T
        real, imag = image[:nz], image[nz:]
        map_real, map_imag = maps[s, 0].astype(F32), maps[s, 1].astype(F32)
        weighted = jnp.concatenate(
            [map_real * real - map_imag * imag, map_real * imag + map_imag * real], 0
        ).astype(BF16)
        halfway = dot(fz[...], weighted).astype(BF16)
        spectrum = dot(halfway, ty[...])
        if s:
            send_sums(s - 1)
        spec_real = spectrum[:nz, :ny] + spectrum[nz:, ny:]
        spec_imag = spectrum[nz:, :ny] - spectrum[:nz, ny:]
        residual = jnp.concatenate(
            [
                sampled * (spec_real - kspace[s, 0].astype(F32)),
                sampled * (spec_imag - kspace[s, 1].astype(F32)),
            ],
            0,
        ).astype(BF16)
        returned = dot(residual, ty[...])
        backward = jnp.concatenate(
            [returned[:nz, :ny] - returned[nz:, ny:], returned[nz:, :ny] + returned[:nz, ny:]], 0
        ).astype(BF16)
        restored = dot(az[...], backward)
        back_real, back_imag = restored[:nz], restored[nz:]
        map_real, map_imag = maps[s, 0].astype(F32), maps[s, 1].astype(F32)
        adjoint = jnp.concatenate(
            [map_real * back_real + map_imag * back_imag, map_real * back_imag - map_imag * back_real], 0
        ).T
        part[s] = adjoint.reshape(chips, 2, rb, width).astype(BF16)
        pair(s).start()
    send_sums(s_local - 1)
    when(active(q), after)

    for d in range(1, peers):
        src = down(d)
        when(
            active(src),
            lambda: remote(
                pen_send.at[0, 0], pen_recv.at[src], p_send_sem.at[d], p_recv_sem.at[d], (e, c, r)
            ).wait_recv(),
        )
    pen_ref[...] = pen_recv[...].reshape(rb, 2 * s_local, zp)

    dc = dc_ref[0]
    for s in range(s_local):
        total = part[s, chip, core].astype(F32) + paired[s, chip].astype(F32)
        for d in range(1, chips):
            src = lax.rem(chip + chips - d, chips)
            remote(
                rs_send.at[s, src], rs_recv.at[s, src], rs_send_sem.at[s, d], rs_recv_sem.at[s, d], (e, partner, r)
            ).wait_recv()
            total = total + rs_recv[s, src].astype(F32)
        adj_ref[:, s * width : (s + 1) * width] = dc * total

    for d in range(chips):
        gather(d).wait_send()
        if d:
            forward(d).wait_send()
            for s in range(s_local):
                scatter(s, d).wait_send()
    for s in range(s_local):
        pair(s).wait_send()
    for d in range(1, peers):
        when(active(up(d)), lambda: window(d).wait_send())
        when(active(q), lambda: penalty_out(d).wait_send())
    pl.when(c < n_c - 1)(lambda: edge_up().wait_send())
    pl.when(c > 0)(lambda: edge_down().wait_send())


def body(kspace, sampling, coil_maps, image, filters, thresholds, dc_weight):
    n_e, n_c, n_r = lax.axis_size("echo"), lax.axis_size("coil"), lax.axis_size("read")
    rb, _, s_local, _, nz = image.shape
    ny = kspace.shape[0]
    peers = n_e * n_r
    rq = window_rows(rb, peers)
    n_q = rb // rq
    zp = -(-(nz + 1) // 128) * 128
    width = 2 * nz
    slices = s_local * n_r
    taps = 2 * slices
    count = filters.shape[0]

    col_cos, col_sin = tables(nz)
    row_cos, row_sin = tables(ny)
    fz = jnp.asarray(np.block([[col_cos, col_sin], [-col_sin, col_cos]]), BF16)
    az = jnp.asarray(np.block([[col_cos, -col_sin], [col_sin, col_cos]]), BF16)
    ty = jnp.asarray(np.concatenate([row_cos, row_sin], 1), BF16)

    rounded = image.astype(BF16)
    flat = rounded.reshape(rb, s_local * width)
    rows = rounded.reshape(rb, 2 * s_local, nz)
    margin = rq + 2
    padded = jnp.pad(rows, ((margin, margin), (0, 0), (0, zp - nz)))
    xs = jnp.stack([padded[j * rq : j * rq + rq + 4] for j in range(n_q + 2)])

    spread = np.zeros((slices, 3, SLAB, 3, 3, 3, 2))
    for at in range(slices):
        for a in range(3):
            for b in range(3):
                for d in range(3):
                    for p in range(2):
                        if 0 <= at + b - 1 < slices:
                            spread[at, a, d * taps + (at + b - 1) * 2 + p, a, b, d, p] = 1.0
    spread = jnp.asarray(spread.reshape(slices, 3 * SLAB, 54), BF16)
    flat_filters = jnp.transpose(filters, (1, 2, 3, 4, 0))
    thr = thresholds[None, :]

    k_view = jnp.transpose(kspace[:, 0, 0], (1, 2, 3, 0))
    m_view = jnp.transpose(coil_maps[:, 0], (1, 2, 3, 0))
    s_view = jnp.transpose(sampling[:, 0], (1, 0))

    k_view, m_view, s_view, fz, az, ty, spread = (
        pltpu.with_memory_space_constraint(x, pltpu.HBM) for x in (k_view, m_view, s_view, fz, az, ty, spread)
    )
    vmem = pl.BlockSpec(memory_space=pltpu.VMEM)
    hbm = pl.BlockSpec(memory_space=pltpu.HBM)
    smem = pl.BlockSpec(memory_space=pltpu.SMEM)
    dma = pltpu.SemaphoreType.DMA
    total, penalty = pl.pallas_call(
        functools.partial(kernel, (n_e, n_c, n_r, n_q, rq, nz, ny)),
        out_shape=(
            jax.ShapeDtypeStruct((rb, s_local * width), F32),
            jax.ShapeDtypeStruct((rb, 2 * s_local, zp), F32),
        ),
        in_specs=[smem, vmem, vmem, hbm, hbm, hbm, hbm, hbm, hbm, vmem, hbm, vmem],
        out_specs=(vmem, vmem),
        scratch_shapes=[
            pltpu.VMEM((n_c, rb, s_local * width), BF16),
            pltpu.VMEM((s_local, n_c // 2, 2, rb, width), BF16),
            pltpu.VMEM((s_local, n_c // 2, rb, width), BF16),
            pltpu.VMEM((s_local, n_c // 2, rb, width), BF16),
            pltpu.VMEM((s_local, n_c // 2, rb, width), BF16),
            pltpu.VMEM((3 * SLAB, slices * count), BF16),
            pltpu.VMEM((slices * count, 3 * SLAB), BF16),
            pltpu.VMEM((slices * count, zp), F32),
            pltpu.VMEM((n_e, n_r, rq + 4, 2 * s_local, zp), BF16),
            pltpu.VMEM((n_e, n_r, rq + 4, 2 * s_local, zp), BF16),
            pltpu.VMEM((n_e, n_r, rq, 2 * s_local, zp), F32),
            pltpu.VMEM((n_q, rq, 2 * s_local, zp), F32),
            pltpu.VMEM((n_e, rq + 4, SLAB, zp), F32),
            pltpu.VMEM((n_e, (rq + 4) * SLAB, zp), BF16),
            pltpu.VMEM(k_view.shape, BF16),
            pltpu.VMEM(m_view.shape, BF16),
            pltpu.VMEM(s_view.shape, jnp.int32),
            pltpu.VMEM(fz.shape, BF16),
            pltpu.VMEM(az.shape, BF16),
            pltpu.VMEM(ty.shape, BF16),
            pltpu.VMEM(spread.shape, BF16),
            dma((7,)),
            dma((n_c,)), dma((n_c,)),
            dma((peers,)), dma((peers,)),
            dma((2,)), dma((peers,)),
            dma((peers,)), dma((peers,)),
            dma((s_local, n_c)), dma((s_local, n_c)),
            dma((n_c,)), dma((n_c,)), dma((s_local,)), dma((s_local,)),
        ],
        compiler_params=pltpu.CompilerParams(
            collective_id=0, has_side_effects=True, vmem_limit_bytes=GRANT
        ),
        name="cascade",
    )(dc_weight, flat, xs, k_view, m_view, s_view, fz, az, ty, flat_filters, spread, thr)
    shape = image.shape
    return image - total.reshape(shape) - penalty[:, :, :nz].reshape(shape)


def solution(mesh):
    return jax.shard_map(
        body,
        mesh=mesh,
        in_specs=(
            P(None, "echo", "coil", "read", None, None),
            P(None, "echo", None),
            P(None, "coil", "read", None, None),
            P("coil", "echo", "read", None, None),
            P(),
            P(),
            P("echo"),
        ),
        out_specs=P("coil", "echo", "read", None, None),
        check_vma=False,
    )
```

profile of v0, /device:TPU:0, one launch (start us, length us, event | category | flops | bytes accessed | tf_op | source)
XLA Modules:
  0.0 30.7 jit_solution(381423335028843065)
XLA Ops:
  0.7 1.0 %convert_element_type.5 = bf16[48,1,2,2,192]{4,3,2,1,0:T(2,128)(2,1)S(1)} convert(f32[48,1,2,2,192]{4,3,2,1,0:T(2,128)} %param.14) | non-fusion elementwise | flops 36864 | bytes 221184 | tf_op jit(solution)/shard_map/convert_element_type | solution.py:364
  1.7 0.1 reshape.12.img_ref
  1.8 0.1 reshape.13
  2.0 0.0 copy-start
  2.0 0.0 copy-start.1
  2.1 0.7 %copy-done = bf16[48,3,3,3,2]{0,4,3,2,1:T(2,128)(2,1)S(1)} copy-done((bf16[48,3,3,3,2]{0,4,3,2,1:T(2,128)(2,1)S(1)}, bf16[48,3,3,3,2]{0,4,3,2,1:T(2,128)(2,1)}, u32[]{:S(2)}) %copy-start) | copy-done | bytes 5208
  2.7 0.0 copy-done.1
  2.7 26.0 %cascade.1 = (f32[48,768]{1,0:T(8,128)S(1)}, f32[48,4,256]{2,1,0:T(4,128)S(1)}) custom-call(f32[1]{0:T(128)S(6)} %copy.19.dc_ref, bf16[48,768]{1,0:T(8,128)(2,1)S(1)} %reshape.12.img_ref, bf16[6,16,4,256]{3,2,1,0:T(4,128)(2,1)S(1)} %fusion.11.xs_ref, bf16[2,2,192,384]{3,2,1,0:T(8,128)(2,1)} %bitcast.45, bf16[2,2,192,384]{3,2,1,0:T(8,128)(2,1)} %bitcast.46, ...), custom_call_target="tpu_custom_call" | custom-call | tf_op jit(solution)/shard_map/cascade/pallas_call | solution.py:394
  28.8 0.2 reshape.15
  28.9 0.0 copy-start.2
  29.0 0.2 reshape.14
  29.1 0.7 %copy-done.2 = f32[48,1,2,2,192]{4,3,2,1,0:T(2,128)S(1)} copy-done((f32[48,1,2,2,192]{4,3,2,1,0:T(2,128)S(1)}, f32[48,1,2,2,192]{4,3,2,1,0:T(2,128)}, u32[]{:S(2)}) %copy-start.2) | copy-done | bytes 147480
  29.9 0.8 %bitcast_subtract_fusion = f32[48,1,2,2,192]{4,3,2,1,0:T(2,128)} fusion(f32[48,1,2,2,192]{4,3,2,0,1:T(2,128)S(1)} %reshape.15, f32[48,1,2,2,192]{4,3,2,1,0:T(2,128)S(1)} %copy-done.2, f32[48,1,2,2,192]{4,3,2,0,1:T(2,128)S(1)} %reshape.14), kind=kLoop, calls=%fused_computation | loop fusion | flops 73728 | bytes 589824 | tf_op jit(solution)/shard_map/sub | solution.py:438
  (6 shorter events, 0.1 us)
Async XLA Ops:
  2.0 0.7 %copy-start = (bf16[48,3,3,3,2]{0,4,3,2,1:T(2,128)(2,1)S(1)}, bf16[48,3,3,3,2]{0,4,3,2,1:T(2,128)(2,1)}, u32[]{:S(2)}) copy-start(bf16[48,3,3,3,2]{0,4,3,2,1:T(2,128)(2,1)} %param.15) | copy-start | bytes 15556
  2.0 0.7 %copy-start.1 = (f32[48]{0:T(128)S(1)}, f32[48]{0:T(128)}, u32[]{:S(2)}) copy-start(f32[48]{0:T(128)} %param.16) | copy-start | bytes 580
  28.9 0.9 %copy-start.2 = (f32[48,1,2,2,192]{4,3,2,1,0:T(2,128)S(1)}, f32[48,1,2,2,192]{4,3,2,1,0:T(2,128)}, u32[]{:S(2)}) copy-start(f32[48,1,2,2,192]{4,3,2,1,0:T(2,128)} %param.14) | copy-start | bytes 442372
where the time goes:
time: 30.9 us; the launch traced here: 30.7 us
  Pallas kernels  26 us (84%)
  local copies, waits for them, and re-layouts  2.1 us (7%)
  other arithmetic  1.84 us (6%)
  between operations  0.74 us (2%)
    pallas_call x1, Pallas kernels, body(): pl.pallas_call(functools.partial(kernel, (n_e, n_c, n_r, n_q, rq, nz, ny)...  26 us
    unnamed x11, local copies, waits for them, and re-layouts  1.53 us
    convert_element_type x1, other arithmetic, body(): rounded = image.astype(BF16)  1 us
    sub x1, other arithmetic, body(): return image - total.reshape(shape) - penalty[:, :, :nz].reshape(shape)  0.84 us

commit v1 on v0

--- a/solution.py
+++ b/solution.py
@@ -35,11 +35,11 @@
 
 def kernel(
     cfg,
-    dc_ref, img_ref, xs_ref, kspace_hbm, maps_hbm, samp_hbm, fz_hbm, az_hbm, ty_hbm,
-    filters_ref, spread_hbm, thr_ref,
-    adj_ref, pen_ref,
+    image_hbm, spread_hbm, filters_hbm, thr_hbm, dc_ref, kspace_hbm, maps_hbm, samp_hbm, fz_hbm, az_hbm, ty_hbm,
+    out_ref,
+    image, flat, padded, spread, filters, thr,
     gat, part, paired, rs_send, rs_recv, wide_ref, tall_ref, level, ext, edge, pen_send, pen_recv, pacc, slab,
-    kspace, maps, samp, fz, az, ty, spread,
+    kspace, maps, samp, fz, az, ty,
     local_sem, ag_send_sem, ag_recv_sem, x_send_sem, x_recv_sem, e_send_sem, e_recv_sem,
     p_send_sem, p_recv_sem, rs_send_sem, rs_recv_sem, f_send_sem, f_recv_sem, pair_send_sem, pair_recv_sem,
 ):
@@ -49,7 +49,7 @@
     c = lax.axis_index("coil")
     r = lax.axis_index("read")
     q = e * n_r + r
-    s_local, rb = rs_send.shape[0], img_ref.shape[0]
+    s_local, rb = rs_send.shape[0], flat.shape[0]
     chips = n_c // 2
     core = lax.rem(c, 2)
     chip = c // 2
@@ -60,7 +60,10 @@
     loads = [
         pltpu.make_async_copy(src, dst, local_sem.at[i])
         for i, (src, dst) in enumerate(
-            [(spread_hbm, spread), (kspace_hbm, kspace), (maps_hbm, maps), (samp_hbm, samp), (fz_hbm, fz), (az_hbm, az), (ty_hbm, ty)]
+            [
+                (image_hbm, image), (spread_hbm, spread), (filters_hbm, filters), (thr_hbm, thr),
+                (maps_hbm, maps), (fz_hbm, fz), (ty_hbm, ty), (kspace_hbm, kspace), (samp_hbm, samp), (az_hbm, az),
+            ]
         )
     ]
 
@@ -100,21 +103,28 @@
                 pl.semaphore_signal(
                     barrier, inc=1, device_id=(up(d) // n_r, c + step, lax.rem(up(d), n_r)), device_id_type=MESH
                 )
+    margin = rq + 2
+    padded[...] = jnp.zeros_like(padded)
+    loads[0].wait()
+    flat[...] = jnp.concatenate([image[:, s, p, :] for s in range(s_local) for p in range(2)], axis=1)
+    gat[c] = flat[...].astype(BF16)
+    padded[margin : margin + rb, :, :nz] = image[...].reshape(rb, 2 * s_local, nz).astype(BF16)
+
     sides = jnp.minimum(c, 1) + jnp.minimum(n_c - 1 - c, 1)
     pl.semaphore_wait(barrier, chips + peers - 1 + peers * sides)
 
     def window(d):
         to = up(d)
         return remote(
-            xs_ref.at[1 + to], ext.at[e, r], x_send_sem.at[d], x_recv_sem.at[d], (to // n_r, c, lax.rem(to, n_r))
+            padded.at[pl.ds((1 + to) * rq, rq + 4)], ext.at[e, r], x_send_sem.at[d], x_recv_sem.at[d], (to // n_r, c, lax.rem(to, n_r))
         )
 
     last = n_q - 1
     edge_up = lambda: remote(
-        xs_ref.at[n_q + 1], edge.at[e, r], e_send_sem.at[0], e_recv_sem.at[q], (0, c + 1, 0)
+        padded.at[pl.ds((n_q + 1) * rq, rq + 4)], edge.at[e, r], e_send_sem.at[0], e_recv_sem.at[q], (0, c + 1, 0)
     )
     edge_down = lambda: remote(
-        xs_ref.at[0], edge.at[e, r], e_send_sem.at[1], e_recv_sem.at[q], (last // n_r, c - 1, last % n_r)
+        padded.at[pl.ds(0, rq + 4)], edge.at[e, r], e_send_sem.at[1], e_recv_sem.at[q], (last // n_r, c - 1, last % n_r)
     )
     for d in range(1, peers):
         when(active(up(d)), lambda: window(d).start())
@@ -123,7 +133,7 @@
 
     def gather(d):
         to = lax.rem(c + 2 * d, n_c) if d else partner
-        return remote(img_ref, gat.at[c], ag_send_sem.at[d], ag_recv_sem.at[d], (e, to, r))
+        return remote(gat.at[c], gat.at[c], ag_send_sem.at[d], ag_recv_sem.at[d], (e, to, r))
 
     def forward(d):
         src = lax.rem(c + n_c - 2 * d, n_c)
@@ -131,19 +141,19 @@
 
     for d in range(chips):
         gather(d).start()
-    gat[c] = img_ref[...]
-
-    count = filters_ref.shape[-1]
+
+    count = filters.shape[-1]
     slices = s_local * n_r
-    flat_filters = filters_ref[...].astype(F32).reshape(-1, count).astype(BF16)
-    loads[0].wait()
+    for load in loads[1:4]:
+        load.wait()
+    flat_filters = filters[...].astype(F32).reshape(-1, count).astype(BF16)
     pieces = [dot(spread[at], flat_filters) for at in range(slices)]
     for at in range(slices):
         wide_ref[:, at * count : (at + 1) * count] = pieces[at].astype(BF16)
         tall_ref[at * count : (at + 1) * count, :] = pieces[at].T.astype(BF16)
     shape = (slices, count, count)
     on = lax.broadcasted_iota(jnp.int32, shape, 1) == lax.broadcasted_iota(jnp.int32, shape, 2)
-    column = jnp.sum(jnp.where(on, thr_ref[...].reshape(1, 1, count), 0.0), axis=2, keepdims=True)
+    column = jnp.sum(jnp.where(on, thr[...].reshape(1, 1, count), 0.0), axis=2, keepdims=True)
     level[...] = jnp.broadcast_to(column, (slices, count, zp)).reshape(slices * count, zp)
 
     has_edge = jnp.logical_or(
@@ -155,18 +165,18 @@
         edge[...] = jnp.zeros_like(edge)
 
     def prepare():
-        ext[e, r] = xs_ref[1 + q]
+        ext[e, r] = padded[pl.ds((1 + q) * rq, rq + 4)]
         for d in range(1, peers):
             src = down(d)
             remote(
-                xs_ref.at[0], ext.at[src // n_r, lax.rem(src, n_r)], x_send_sem.at[d], x_recv_sem.at[d], (e, c, r)
+                padded.at[pl.ds(0, rq + 4)], ext.at[src // n_r, lax.rem(src, n_r)], x_send_sem.at[d], x_recv_sem.at[d], (e, c, r)
             ).wait_recv()
 
         @pl.when(has_edge)
         def _():
             for src in range(peers):
                 remote(
-                    xs_ref.at[0], edge.at[src // n_r, src % n_r], e_send_sem.at[0], e_recv_sem.at[src], (e, c, r)
+                    padded.at[pl.ds(0, rq + 4)], edge.at[src // n_r, src % n_r], e_send_sem.at[0], e_recv_sem.at[src], (e, c, r)
                 ).wait_recv()
 
         rows = rq + 4
@@ -243,13 +253,13 @@
 
     for d in range(1, chips):
         src = lax.rem(c + n_c - 2 * d, n_c)
-        remote(img_ref, gat.at[src], ag_send_sem.at[d], ag_recv_sem.at[d], (e, partner, r)).wait_recv()
+        remote(gat.at[src], gat.at[src], ag_send_sem.at[d], ag_recv_sem.at[d], (e, partner, r)).wait_recv()
         forward(d).start()
-    remote(img_ref, gat.at[partner], ag_send_sem.at[0], ag_recv_sem.at[0], (e, partner, r)).wait_recv()
+    remote(gat.at[partner], gat.at[partner], ag_send_sem.at[0], ag_recv_sem.at[0], (e, partner, r)).wait_recv()
     for d in range(1, chips):
         src = lax.rem(partner + n_c - 2 * d, n_c)
         remote(gat.at[src], gat.at[src], f_send_sem.at[d], f_recv_sem.at[d], (e, partner, r)).wait_recv()
-    for load in loads[1:]:
+    for load in loads[4:]:
         load.wait()
 
     def pair(s):
@@ -314,9 +324,8 @@
                 pen_send.at[0, 0], pen_recv.at[src], p_send_sem.at[d], p_recv_sem.at[d], (e, c, r)
             ).wait_recv(),
         )
-    pen_ref[...] = pen_recv[...].reshape(rb, 2 * s_local, zp)
-
-    dc = dc_ref[0]
+    held = pen_recv[...].reshape(rb, 2 * s_local, zp)
+    base = flat[...] - jnp.concatenate([held[:, k, :nz] for k in range(2 * s_local)], axis=1)
     for s in range(s_local):
         total = part[s, chip, core].astype(F32) + paired[s, chip].astype(F32)
         for d in range(1, chips):
@@ -325,7 +334,7 @@
                 rs_send.at[s, src], rs_recv.at[s, src], rs_send_sem.at[s, d], rs_recv_sem.at[s, d], (e, partner, r)
             ).wait_recv()
             total = total + rs_recv[s, src].astype(F32)
-        adj_ref[:, s * width : (s + 1) * width] = dc * total
+        out_ref[:, s * width : (s + 1) * width] = base[:, s * width : (s + 1) * width] - dc_ref[0] * total
 
     for d in range(chips):
         gather(d).wait_send()
@@ -361,13 +370,6 @@
     az = jnp.asarray(np.block([[col_cos, -col_sin], [col_sin, col_cos]]), BF16)
     ty = jnp.asarray(np.concatenate([row_cos, row_sin], 1), BF16)
 
-    rounded = image.astype(BF16)
-    flat = rounded.reshape(rb, s_local * width)
-    rows = rounded.reshape(rb, 2 * s_local, nz)
-    margin = rq + 2
-    padded = jnp.pad(rows, ((margin, margin), (0, 0), (0, zp - nz)))
-    xs = jnp.stack([padded[j * rq : j * rq + rq + 4] for j in range(n_q + 2)])
-
     spread = np.zeros((slices, 3, SLAB, 3, 3, 3, 2))
     for at in range(slices):
         for a in range(3):
@@ -377,29 +379,34 @@
                         if 0 <= at + b - 1 < slices:
                             spread[at, a, d * taps + (at + b - 1) * 2 + p, a, b, d, p] = 1.0
     spread = jnp.asarray(spread.reshape(slices, 3 * SLAB, 54), BF16)
-    flat_filters = jnp.transpose(filters, (1, 2, 3, 4, 0))
-    thr = thresholds[None, :]
 
     k_view = jnp.transpose(kspace[:, 0, 0], (1, 2, 3, 0))
     m_view = jnp.transpose(coil_maps[:, 0], (1, 2, 3, 0))
     s_view = jnp.transpose(sampling[:, 0], (1, 0))
 
-    k_view, m_view, s_view, fz, az, ty, spread = (
-        pltpu.with_memory_space_constraint(x, pltpu.HBM) for x in (k_view, m_view, s_view, fz, az, ty, spread)
+    operands = tuple(
+        pltpu.with_memory_space_constraint(x, pltpu.HBM)
+        for x in (
+            image[:, 0], spread, jnp.transpose(filters, (1, 2, 3, 4, 0)), thresholds[None, :],
+            k_view, m_view, s_view, fz, az, ty,
+        )
     )
     vmem = pl.BlockSpec(memory_space=pltpu.VMEM)
     hbm = pl.BlockSpec(memory_space=pltpu.HBM)
     smem = pl.BlockSpec(memory_space=pltpu.SMEM)
     dma = pltpu.SemaphoreType.DMA
-    total, penalty = pl.pallas_call(
+    updated = pl.pallas_call(
         functools.partial(kernel, (n_e, n_c, n_r, n_q, rq, nz, ny)),
-        out_shape=(
-            jax.ShapeDtypeStruct((rb, s_local * width), F32),
-            jax.ShapeDtypeStruct((rb, 2 * s_local, zp), F32),
-        ),
-        in_specs=[smem, vmem, vmem, hbm, hbm, hbm, hbm, hbm, hbm, vmem, hbm, vmem],
-        out_specs=(vmem, vmem),
+        out_shape=jax.ShapeDtypeStruct((rb, s_local * width), F32),
+        in_specs=[hbm] * 4 + [smem] + [hbm] * 6,
+        out_specs=vmem,
         scratch_shapes=[
+            pltpu.VMEM((rb, s_local, 2, nz), F32),
+            pltpu.VMEM((rb, s_local * width), F32),
+            pltpu.VMEM((rb + 2 * (rq + 2), 2 * s_local, zp), BF16),
+            pltpu.VMEM(spread.shape, BF16),
+            pltpu.VMEM((3, 3, 3, 2, count), BF16),
+            pltpu.VMEM((1, count), F32),
             pltpu.VMEM((n_c, rb, s_local * width), BF16),
             pltpu.VMEM((s_local, n_c // 2, 2, rb, width), BF16),
             pltpu.VMEM((s_local, n_c // 2, rb, width), BF16),
@@ -420,8 +427,7 @@
             pltpu.VMEM(fz.shape, BF16),
             pltpu.VMEM(az.shape, BF16),
             pltpu.VMEM(ty.shape, BF16),
-            pltpu.VMEM(spread.shape, BF16),
-            dma((7,)),
+            dma((10,)),
             dma((n_c,)), dma((n_c,)),
             dma((peers,)), dma((peers,)),
             dma((2,)), dma((peers,)),
@@ -433,9 +439,8 @@
             collective_id=0, has_side_effects=True, vmem_limit_bytes=GRANT
         ),
         name="cascade",
-    )(dc_weight, flat, xs, k_view, m_view, s_view, fz, az, ty, flat_filters, spread, thr)
-    shape = image.shape
-    return image - total.reshape(shape) - penalty[:, :, :nz].reshape(shape)
+    )(*operands[:4], dc_weight, *operands[4:])
+    return updated.reshape(image.shape)
 
 
 def solution(mesh):

time: 30.9 us -> 28.1 us (0.909)
  other arithmetic: 1.84 us -> 0 us
  local copies, waits for them, and re-layouts: 2.1 us -> 0.87 us
  Pallas kernels: 26 us -> 26.5 us
    unnamed x11 -> x0, local copies, waits for them, and re-layouts: 1.53 us -> none
    convert_element_type x1 -> x0, other arithmetic: 1 us -> none  [body(): rounded = image.astype(BF16)]
    sub x1 -> x0, other arithmetic: 0.84 us -> none  [body(): return image - total.reshape(shape) - penalty[:, :, :nz].reshape(shape)]
    pallas_call x1, Pallas kernels: 26 us -> 26.5 us  [body(): pl.pallas_call(functools.partial(kernel, (n_e, n_c, n_r, n_q, rq, nz, ny)...]
    reshape x4 -> x1, local copies, waits for them, and re-layouts: 0.55 us -> 0.87 us  [body(): return updated.reshape(image.shape)]
where the time goes in v1:
time: 28.1 us; the launch traced here: 28 us
  Pallas kernels  26.5 us (94%)
  local copies, waits for them, and re-layouts  0.87 us (3%)
  between operations  0.66 us (2%)
    pallas_call x1, Pallas kernels, body(): pl.pallas_call(functools.partial(kernel, (n_e, n_c, n_r, n_q, rq, nz, ny)...  26.5 us
    reshape x1, local copies, waits for them, and re-layouts, body(): return updated.reshape(image.shape)  0.87 us

profile of v1, /device:TPU:0, one launch (start us, length us, event | category | flops | bytes accessed | tf_op | source)
XLA Modules:
  0.0 28.0 jit_solution(10784219617626866853)
XLA Ops:
  0.7 26.5 %cascade.1 = f32[48,768]{1,0:T(8,128)S(1)} custom-call(f32[48,2,2,192]{3,2,1,0:T(2,128)} %bitcast.16, bf16[4,96,54]{2,1,0:T(8,128)(2,1)} %constant.11.clone.spread_hbm, bf16[3,3,3,2,48]{4,3,2,1,0:T(2,128)(2,1)} %bitcast.17, f32[1,48]{1,0:T(1,128)} %bitcast.18, f32[1]{0:T(128)S(6)} %copy.13.dc_ref, bf16[2,2,192,384]{3,2,1,0:T(8,128)(2,1)} %bitcast.13, ...), custom_call_target="tpu_custom_call" | custom-call | tf_op jit(solution)/shard_map/cascade/pallas_call | solution.py:398
  27.1 0.9 %reshape.3 = f32[48,1,2,2,192]{4,3,2,0,1:T(2,128)} reshape(f32[48,768]{1,0:T(8,128)S(1)} %cascade.1) | data formatting | bytes 294912 | tf_op jit(solution)/shard_map/reshape | solution.py:443

commit v2 on v1

v2 whole, which is shorter than its diff:
```python
import functools

import numpy as np
import jax
import jax.numpy as jnp
from jax import lax
from jax.experimental import pallas as pl
from jax.experimental.pallas import tpu as pltpu
from jax.sharding import PartitionSpec as P

MESH = pl.DeviceIdType.MESH
F32 = jnp.float32
BF16 = jnp.bfloat16
SLAB = 32
GRANT = 24 << 20
TINY = float(np.finfo(np.float32).tiny)
SPLITS = (3, 8, 10, 11)


def tables(length):
    product = np.outer(np.arange(length), np.arange(length)) % length
    phases = product * (2.0 * np.pi / length)
    normalize = length ** (-0.5)
    return np.cos(phases) * normalize, np.sin(phases) * normalize


def window_rows(rows, peers):
    for size in range(2, rows + 1):
        if rows % size == 0 and rows // size <= peers:
            return size
    return rows


def dot(left, right):
    return jnp.dot(left, right, preferred_element_type=F32)


def kernel(
    cfg,
    image_hbm, spread_hbm, filters_hbm, thr_hbm, dc_ref, kspace_hbm, maps_hbm, samp_hbm, fz_hbm, az_hbm, ty_hbm,
    out_ref,
    image, flat, padded, spread, filters, thr,
    gat, part, paired, rs_send, rs_recv, wide_ref, tall_ref, level, ext, edge, pen_send, pen_recv, pacc, slab,
    kspace, maps, samp, fz, az, ty, k_rows, m_rows, s_rows, weighted, stack,
    local_sem, ag_send_sem, ag_recv_sem, x_send_sem, x_recv_sem, e_send_sem, e_recv_sem,
    p_send_sem, p_recv_sem, rs_send_sem, rs_recv_sem, f_send_sem, f_recv_sem, pair_send_sem, pair_recv_sem,
):
    n_e, n_c, n_r, n_q, rq, nz, ny = cfg
    peers = n_e * n_r
    e = lax.axis_index("echo")
    c = lax.axis_index("coil")
    r = lax.axis_index("read")
    q = e * n_r + r
    s_local, rb = rs_send.shape[0], flat.shape[0]
    chips = n_c // 2
    core = lax.rem(c, 2)
    chip = c // 2
    partner = c + 1 - 2 * core
    width = 2 * nz
    zp = ext.shape[-1]
    half = ny // 2
    group = chips // 2
    side = jnp.where(chip < group, 1, 0)

    loads = [
        pltpu.make_async_copy(src, dst, local_sem.at[i])
        for i, (src, dst) in enumerate(
            [
                (image_hbm, image), (spread_hbm, spread), (filters_hbm, filters), (thr_hbm, thr),
                (maps_hbm, maps), (fz_hbm, fz), (ty_hbm, ty), (kspace_hbm, kspace), (samp_hbm, samp), (az_hbm, az),
            ]
        )
    ]

    for load in loads:
        load.start()

    def remote(src, dst, send, recv, target):
        return pltpu.make_async_remote_copy(
            src_ref=src, dst_ref=dst, send_sem=send, recv_sem=recv, device_id=target, device_id_type=MESH
        )

    def when(condition, act):
        if condition is True:
            act()
        else:
            pl.when(condition)(act)

    def up(d):
        return lax.rem(q + d, peers)

    def down(d):
        return lax.rem(q + peers - d, peers)

    def active(which):
        return True if n_q == peers else which < n_q

    barrier = pltpu.get_barrier_semaphore()
    for d in range(chips):
        to = lax.rem(c + 2 * d, n_c) if d else partner
        pl.semaphore_signal(barrier, inc=1, device_id=(e, to, r), device_id_type=MESH)
    for d in range(peers):
        if d:
            pl.semaphore_signal(barrier, inc=1, device_id=(up(d) // n_r, c, lax.rem(up(d), n_r)), device_id_type=MESH)
        for step, ok in ((1, c < n_c - 1), (-1, c > 0)):
            @pl.when(ok)
            def _():
                pl.semaphore_signal(
                    barrier, inc=1, device_id=(up(d) // n_r, c + step, lax.rem(up(d), n_r)), device_id_type=MESH
                )
    margin = rq + 2
    loads[0].wait()
    flat[...] = jnp.concatenate([image[:, s, p, :] for s in range(s_local) for p in range(2)], axis=1)
    for s in range(s_local):
        gat[s, c] = flat[:, s * width : (s + 1) * width].astype(BF16)

    sides = jnp.minimum(c, 1) + jnp.minimum(n_c - 1 - c, 1)
    pl.semaphore_wait(barrier, chips + peers - 1 + peers * sides)

    def window(d):
        to = up(d)
        return remote(
            padded.at[pl.ds((1 + to) * rq, rq + 4)], ext.at[e, r], x_send_sem.at[d], x_recv_sem.at[d], (to // n_r, c, lax.rem(to, n_r))
        )

    last = n_q - 1
    def edge_up():
        return remote(
            padded.at[pl.ds(margin + rb - 2, 2)], edge.at[0, e, r], e_send_sem.at[0], e_recv_sem.at[0, q], (0, c + 1, 0)
        )

    def edge_down():
        return remote(
            padded.at[pl.ds(margin, 2)], edge.at[1, e, r], e_send_sem.at[1], e_recv_sem.at[1, q],
            (last // n_r, c - 1, last % n_r),
        )

    def gather(s, d):
        to = lax.rem(c + 2 * d, n_c) if d is not None else partner
        at = 0 if d is None else d
        return remote(gat.at[s, c], gat.at[s, c], ag_send_sem.at[s, at], ag_recv_sem.at[s, at], (e, to, r))

    def gathered(s, d):
        src = lax.rem(c + n_c - 2 * d, n_c)
        return remote(gat.at[s, src], gat.at[s, src], ag_send_sem.at[s, d], ag_recv_sem.at[s, d], (e, partner, r))

    def forward(s, d):
        src = lax.rem(c + n_c - 2 * d, n_c)
        return remote(gat.at[s, src], gat.at[s, src], f_send_sem.at[s, d], f_recv_sem.at[s, d], (e, partner, r))

    def targets(act, dists):
        for dist in dists:
            pl.when(chip + dist < chips)(lambda: act(dist))
            pl.when(chip - dist >= 0)(lambda: act(chips - dist))

    def relay(s, dists):
        def one(d):
            gathered(s, d).wait_recv()
            forward(s, d).start()

        for dist in dists:
            pl.when(chip - dist >= 0)(lambda: one(dist))
            pl.when(chip + dist < chips)(lambda: one(chips - dist))

    near = range(1, chips)
    far = near[::-1]

    padded[...] = jnp.zeros_like(padded)
    padded[margin : margin + rb, :, :nz] = image[...].reshape(rb, 2 * s_local, nz).astype(BF16)
    for d in range(1, peers):
        when(active(up(d)), lambda: window(d).start())
    pl.when(c < n_c - 1)(lambda: edge_up().start())
    pl.when(c > 0)(lambda: edge_down().start())
    for s in range(s_local):
        targets(lambda d: gather(s, d).start(), near if s else far)
        gather(s, None).start()

    def complete(s):
        remote(
            gat.at[s, partner], gat.at[s, partner], ag_send_sem.at[s, 0], ag_recv_sem.at[s, 0], (e, partner, r)
        ).wait_recv()
        for d in range(1, chips):
            src = lax.rem(partner + n_c - 2 * d, n_c)
            remote(
                gat.at[s, src], gat.at[s, src], f_send_sem.at[s, d], f_recv_sem.at[s, d], (e, partner, r)
            ).wait_recv()

    count = filters.shape[-1]
    slices = s_local * n_r
    for load in loads[1:4]:
        load.wait()
    flat_filters = filters[...].astype(F32).reshape(-1, count).astype(BF16)
    pieces = [dot(spread[at], flat_filters) for at in range(slices)]
    for at in range(slices):
        wide_ref[:, at * count : (at + 1) * count] = pieces[at].astype(BF16)
        tall_ref[at * count : (at + 1) * count, :] = pieces[at].T.astype(BF16)
    shape = (slices, count, count)
    on = lax.broadcasted_iota(jnp.int32, shape, 1) == lax.broadcasted_iota(jnp.int32, shape, 2)
    column = jnp.sum(jnp.where(on, thr[...].reshape(1, 1, count), 0.0), axis=2, keepdims=True)
    level[...] = jnp.broadcast_to(column, (slices, count, zp)).reshape(slices * count, zp)

    def prepare():
        ext[e, r] = padded[pl.ds((1 + q) * rq, rq + 4)]
        for d in range(1, peers):
            src = down(d)
            remote(
                padded.at[pl.ds(0, rq + 4)], ext.at[src // n_r, lax.rem(src, n_r)], x_send_sem.at[d], x_recv_sem.at[d], (e, c, r)
            ).wait_recv()

        def border(which, begin):
            for src in range(peers):
                at = (which, src // n_r, src % n_r)
                remote(
                    padded.at[pl.ds(0, 2)], edge.at[at], e_send_sem.at[0], e_recv_sem.at[which, src], (e, c, r)
                ).wait_recv()
                ext[src // n_r, src % n_r, begin : begin + 2] = edge[at]

        pl.when(jnp.logical_and(q == 0, c > 0))(lambda: border(0, 0))
        pl.when(jnp.logical_and(q == last, c < n_c - 1))(lambda: border(1, rq + 2))

        rows = rq + 4
        taps = 2 * s_local * n_r
        for echo in range(n_e):
            parts = [ext[echo, read].astype(F32) for read in range(n_r)]
            block = jnp.concatenate(parts, axis=1) if n_r > 1 else parts[0]
            flat = block.reshape(rows * taps, zp)
            moved = [
                pltpu.roll(flat, 1, 1).reshape(rows, taps, zp),
                block,
                pltpu.roll(flat, zp - 1, 1).reshape(rows, taps, zp),
            ]
            fill = [jnp.zeros((rows, SLAB - 3 * taps, zp), F32)] if SLAB > 3 * taps else []
            slab[echo] = jnp.concatenate(moved + fill, axis=1).reshape(rows * SLAB, zp).astype(BF16)

        pacc[...] = jnp.zeros_like(pacc)

    def respond(begin, end):
        tall = tall_ref[...]
        wide = wide_ref[...]
        first = c * rb + q * rq - 1

        for i in range(begin, end):
            window = slice(i * SLAB, (i + 3) * SLAB)
            response = [dot(tall, slab[echo, window, :]) for echo in range(n_e)]
            energy = response[0] * response[0]
            for other in response[1:]:
                energy = energy + other * other
            factor = 1.0 / (1.0 + level[...] * lax.rsqrt(jnp.maximum(energy, TINY)))
            if i in (0, rq + 1):
                inside = jnp.logical_and(first + i >= 0, first + i < ny)
                factor = jnp.where(inside, factor, 0.0)
            for echo in range(n_e):
                spread = dot(wide, (response[echo] * factor).astype(BF16))
                for a in range(3):
                    pacc[echo, i + a] += spread[a * SLAB : (a + 1) * SLAB]

    def collect():
        taps = 2 * s_local * n_r
        lane = lax.broadcasted_iota(jnp.int32, (1, 1, zp), 2)
        for echo in range(n_e):
            held = pacc[echo, 2 : 2 + rq]
            low = pltpu.roll(held[:, :taps].reshape(rq * taps, zp), zp - 1, 1).reshape(rq, taps, zp)
            high = pltpu.roll(held[:, 2 * taps : 3 * taps].reshape(rq * taps, zp), 1, 1).reshape(rq, taps, zp)
            low = jnp.where(lane < nz - 1, low, 0.0)
            high = jnp.where(lane > 0, high, 0.0)
            total = low + held[:, taps : 2 * taps] + high
            for read in range(n_r):
                pen_send[echo, read] = total[:, read * 2 * s_local : (read + 1) * 2 * s_local].astype(BF16)
        pen_recv[q] = pen_send[e, r]

    def penalty_out(d):
        to = up(d)
        return remote(
            pen_send.at[to // n_r, lax.rem(to, n_r)], pen_recv.at[q], p_send_sem.at[d], p_recv_sem.at[d],
            (to // n_r, c, lax.rem(to, n_r)),
        )

    marks = [0] + [(rq + 2) * part // 14 for part in SPLITS] + [rq + 2]

    def rows(at):
        def act():
            if at == 0:
                prepare()
            respond(marks[at], marks[at + 1])
            if at == len(marks) - 2:
                collect()
                for d in range(1, peers):
                    penalty_out(d).start()

        when(active(q), act)

    def turn():
        for load in loads[4:]:
            load.wait()
        for buf in (k_rows, m_rows, weighted):
            buf[...] = jnp.zeros_like(buf)
        for s in range(s_local):
            for p in range(2):
                at = slice(p * zp, p * zp + nz)
                k_rows[s, :, at] = kspace[s, p].astype(F32).T.astype(BF16)
                m_rows[s, :, at] = maps[s, p].astype(F32).T.astype(BF16)
        s_rows[:, :nz] = samp[...].astype(F32).T
        s_rows[:, nz:] = jnp.zeros((ny, zp - nz), F32)

    def halves(j):
        return side if j == 0 else 1 - side

    def pair(s, j):
        h = halves(j)
        return remote(
            part.at[s, h, :, 1 - core], paired.at[s, h], pair_send_sem.at[s, j], pair_recv_sem.at[s, j],
            (e, partner, r),
        )

    def scatter(s, to):
        d = lax.rem(to - chip + chips, chips)
        return remote(
            rs_send.at[s, to], rs_recv.at[s, chip], rs_send_sem.at[s, d], rs_recv_sem.at[s, d],
            (e, 2 * to + core, r),
        )

    def send_sums(s, j):
        pair(s, j).wait_recv()
        h = halves(j)
        sums = (part[s, h, :, core].astype(F32) + paired[s, h].astype(F32)).astype(BF16)
        for k in range(group):
            to = h * group + k
            rs_send[s, to] = sums[k]
            if j:
                pl.when(to != chip)(lambda: scatter(s, to).start())
            else:
                scatter(s, to).start()

    def swapped(x, sign):
        low, high = x[:, :zp], x[:, zp:]
        return jnp.concatenate([high, -low] if sign > 0 else [-high, low], axis=1)

    def columns(s, which):
        starts = [pl.multiple_of((2 * k + which) * rb, 8) for k in range(chips)]
        image = jnp.concatenate([gat[s, 2 * k + which] for k in range(chips)], axis=0)
        sense = jnp.concatenate([m_rows[s, pl.ds(at, rb), :] for at in starts], axis=0)
        real, imag = image[:, :nz].astype(F32), image[:, nz:].astype(F32)
        map_real, map_imag = sense[:, :nz].astype(F32), sense[:, zp : zp + nz].astype(F32)
        weighted[:half, :nz] = (map_real * real - map_imag * imag).astype(BF16)
        weighted[:half, zp : zp + nz] = (map_real * imag + map_imag * real).astype(BF16)
        halfway = dot(weighted[:half, :], fz[...])
        upper, lower = halfway.astype(BF16), swapped(halfway, 1).astype(BF16)
        for k, at in enumerate(starts):
            stack[pl.ds(at, rb), :] = upper[k * rb : (k + 1) * rb]
            stack[pl.ds(ny + at, rb), :] = lower[k * rb : (k + 1) * rb]

    def fronts(s):
        spectrum = dot(ty[...], stack[...])
        sampled = s_rows[...]
        sampled = jnp.concatenate([sampled, sampled], axis=1)
        residual = sampled * (spectrum - k_rows[s].astype(F32))
        stack[:ny] = residual.astype(BF16)
        stack[ny:] = swapped(residual, -1).astype(BF16)

    def middle():
        weighted[...] = dot(ty[...], stack[...]).astype(BF16)

    def backs(s, j):
        h = halves(j)
        at = pl.ds(pl.multiple_of(h * half, 16), half)
        restored = dot(weighted[at, :], az[...])
        back_real, back_imag = restored[:, :nz], restored[:, zp : zp + nz]
        map_real, map_imag = m_rows[s, at, :nz].astype(F32), m_rows[s, at, zp : zp + nz].astype(F32)
        adjoint = jnp.concatenate(
            [
                (map_real * back_real + map_imag * back_imag).astype(BF16),
                (map_real * back_imag - map_imag * back_real).astype(BF16),
            ],
            axis=1,
        )
        part[s, h] = adjoint.reshape(group, 2, rb, width)
        pair(s, j).start()

    turn()
    rows(0)
    rows(1)
    relay(0, near)
    columns(0, core)
    complete(0)
    columns(0, 1 - core)
    fronts(0)
    middle()
    relay(1, near)
    backs(0, 0)
    backs(0, 1)
    columns(1, core)
    send_sums(0, 0)
    complete(1)
    columns(1, 1 - core)
    send_sums(0, 1)
    fronts(1)
    middle()
    backs(1, 0)
    backs(1, 1)
    rows(2)
    send_sums(1, 0)
    rows(3)
    send_sums(1, 1)
    rows(4)

    def wait_pen():
        for d in range(1, peers):
            src = down(d)
            when(
                active(src),
                lambda: remote(
                    pen_send.at[0, 0], pen_recv.at[src], p_send_sem.at[d], p_recv_sem.at[d], (e, c, r)
                ).wait_recv(),
            )
        held = pen_recv[...].astype(F32).reshape(rb, 2 * s_local, zp)
        flat[...] = flat[...] - jnp.concatenate([held[:, k, :nz] for k in range(2 * s_local)], axis=1)

    def hops(s):
        for d in range(1, chips):
            src = lax.rem(chip + chips - d, chips)
            remote(
                rs_send.at[s, src], rs_recv.at[s, src], rs_send_sem.at[s, d], rs_recv_sem.at[s, d], (e, partner, r)
            ).wait_recv()

    def finish(s):
        mine, slot = chip // group, lax.rem(chip, group)
        total = part[s, mine, slot, core].astype(F32) + paired[s, mine, slot].astype(F32)
        for d in range(1, chips):
            total = total + rs_recv[s, lax.rem(chip + chips - d, chips)].astype(F32)
        at = slice(s * width, (s + 1) * width)
        out_ref[:, at] = flat[:, at] - dc_ref[0] * total

    wait_pen()
    for s in range(s_local):
        hops(s)
        finish(s)

    for s in range(s_local):
        gather(s, None).wait_send()
        for d in range(1, chips):
            gather(s, d).wait_send()
            forward(s, d).wait_send()
            scatter(s, lax.rem(chip + d, chips)).wait_send()
    for s in range(s_local):
        for j in range(2):
            pair(s, j).wait_send()
    for d in range(1, peers):
        when(active(up(d)), lambda: window(d).wait_send())
        when(active(q), lambda: penalty_out(d).wait_send())
    pl.when(c < n_c - 1)(lambda: edge_up().wait_send())
    pl.when(c > 0)(lambda: edge_down().wait_send())


def body(kspace, sampling, coil_maps, image, filters, thresholds, dc_weight):
    n_e, n_c, n_r = lax.axis_size("echo"), lax.axis_size("coil"), lax.axis_size("read")
    rb, _, s_local, _, nz = image.shape
    ny = kspace.shape[0]
    peers = n_e * n_r
    rq = window_rows(rb, peers)
    n_q = rb // rq
    zp = -(-(nz + 1) // 128) * 128
    width = 2 * nz
    slices = s_local * n_r
    taps = 2 * slices
    count = filters.shape[0]

    col_cos, col_sin = tables(nz)
    row_cos, row_sin = tables(ny)
    gap = ((0, zp - nz), (0, zp - nz))
    col_cos, col_sin = np.pad(col_cos, gap), np.pad(col_sin, gap)
    fz = jnp.asarray(np.block([[col_cos, -col_sin], [col_sin, col_cos]]), BF16)
    az = jnp.asarray(np.block([[col_cos, col_sin], [-col_sin, col_cos]]), BF16)
    ty = jnp.asarray(np.concatenate([row_cos, row_sin], 1), BF16)

    spread = np.zeros((slices, 3, SLAB, 3, 3, 3, 2))
    for at in range(slices):
        for a in range(3):
            for b in range(3):
                for d in range(3):
                    for p in range(2):
                        if 0 <= at + b - 1 < slices:
                            spread[at, a, d * taps + (at + b - 1) * 2 + p, a, b, d, p] = 1.0
    spread = jnp.asarray(spread.reshape(slices, 3 * SLAB, 54), BF16)

    k_view = jnp.transpose(kspace[:, 0, 0], (1, 2, 3, 0))
    m_view = jnp.transpose(coil_maps[:, 0], (1, 2, 3, 0))
    s_view = jnp.transpose(sampling[:, 0], (1, 0))

    operands = tuple(
        pltpu.with_memory_space_constraint(x, pltpu.HBM)
        for x in (
            image[:, 0], spread, jnp.transpose(filters, (1, 2, 3, 4, 0)), thresholds[None, :],
            k_view, m_view, s_view, fz, az, ty,
        )
    )
    vmem = pl.BlockSpec(memory_space=pltpu.VMEM)
    hbm = pl.BlockSpec(memory_space=pltpu.HBM)
    smem = pl.BlockSpec(memory_space=pltpu.SMEM)
    dma = pltpu.SemaphoreType.DMA
    updated = pl.pallas_call(
        functools.partial(kernel, (n_e, n_c, n_r, n_q, rq, nz, ny)),
        out_shape=jax.ShapeDtypeStruct((rb, s_local * width), F32),
        in_specs=[hbm] * 4 + [smem] + [hbm] * 6,
        out_specs=vmem,
        scratch_shapes=[
            pltpu.VMEM((rb, s_local, 2, nz), F32),
            pltpu.VMEM((rb, s_local * width), F32),
            pltpu.VMEM((rb + 2 * (rq + 2), 2 * s_local, zp), BF16),
            pltpu.VMEM(spread.shape, BF16),
            pltpu.VMEM((3, 3, 3, 2, count), BF16),
            pltpu.VMEM((1, count), F32),
            pltpu.VMEM((s_local, n_c, rb, width), BF16),
            pltpu.VMEM((s_local, 2, n_c // 4, 2, rb, width), BF16),
            pltpu.VMEM((s_local, 2, n_c // 4, rb, width), BF16),
            pltpu.VMEM((s_local, n_c // 2, rb, width), BF16),
            pltpu.VMEM((s_local, n_c // 2, rb, width), BF16),
            pltpu.VMEM((3 * SLAB, slices * count), BF16),
            pltpu.VMEM((slices * count, 3 * SLAB), BF16),
            pltpu.VMEM((slices * count, zp), F32),
            pltpu.VMEM((n_e, n_r, rq + 4, 2 * s_local, zp), BF16),
            pltpu.VMEM((2, n_e, n_r, 2, 2 * s_local, zp), BF16),
            pltpu.VMEM((n_e, n_r, rq, 2 * s_local, zp), BF16),
            pltpu.VMEM((n_q, rq, 2 * s_local, zp), BF16),
            pltpu.VMEM((n_e, rq + 4, SLAB, zp), F32),
            pltpu.VMEM((n_e, (rq + 4) * SLAB, zp), BF16),
            pltpu.VMEM(k_view.shape, BF16),
            pltpu.VMEM(m_view.shape, BF16),
            pltpu.VMEM(s_view.shape, jnp.int32),
            pltpu.VMEM(fz.shape, BF16),
            pltpu.VMEM(az.shape, BF16),
            pltpu.VMEM(ty.shape, BF16),
            pltpu.VMEM((s_local, ny, 2 * zp), BF16),
            pltpu.VMEM((s_local, ny, 2 * zp), BF16),
            pltpu.VMEM((ny, zp), F32),
            pltpu.VMEM((ny, 2 * zp), BF16),
            pltpu.VMEM((2 * ny, 2 * zp), BF16),
            dma((10,)),
            dma((s_local, n_c)), dma((s_local, n_c)),
            dma((peers,)), dma((peers,)),
            dma((2,)), dma((2, peers)),
            dma((peers,)), dma((peers,)),
            dma((s_local, n_c)), dma((s_local, n_c)),
            dma((s_local, n_c)), dma((s_local, n_c)), dma((s_local, 2)), dma((s_local, 2)),
        ],
        compiler_params=pltpu.CompilerParams(
            collective_id=0, has_side_effects=True, vmem_limit_bytes=GRANT
        ),
        name="cascade",
    )(*operands[:4], dc_weight, *operands[4:])
    return updated.reshape(image.shape)


def solution(mesh):
    return jax.shard_map(
        body,
        mesh=mesh,
        in_specs=(
            P(None, "echo", "coil", "read", None, None),
            P(None, "echo", None),
            P(None, "coil", "read", None, None),
            P("coil", "echo", "read", None, None),
            P(),
            P(),
            P("echo"),
        ),
        out_specs=P("coil", "echo", "read", None, None),
        check_vma=False,
    )
```

time: 28.1 us -> 26.7 us (0.950)
  Pallas kernels: 26.5 us -> 25 us
    pallas_call x1, Pallas kernels: 26.5 us -> 25 us  [body(): pl.pallas_call(functools.partial(kernel, (n_e, n_c, n_r, n_q, rq, nz, ny)...]
where the time goes in v2:
time: 26.7 us; the launch traced here: 26.6 us
  Pallas kernels  25 us (94%)
  local copies, waits for them, and re-layouts  0.87 us (3%)
  between operations  0.66 us (2%)
    pallas_call x1, Pallas kernels, body(): pl.pallas_call(functools.partial(kernel, (n_e, n_c, n_r, n_q, rq, nz, ny)...  25 us
    reshape x1, local copies, waits for them, and re-layouts, body(): return updated.reshape(image.shape)  0.87 us

profile of v2, /device:TPU:0, one launch (start us, length us, event | category | flops | bytes accessed | tf_op | source)
XLA Modules:
  0.0 26.6 jit_solution(11868755598546625647)
XLA Ops:
  0.7 25.0 %cascade.1 = f32[48,768]{1,0:T(8,128)S(1)} custom-call(f32[48,2,2,192]{3,2,1,0:T(2,128)} %bitcast.16, bf16[4,96,54]{2,1,0:T(8,128)(2,1)} %constant.11.clone.spread_hbm, bf16[3,3,3,2,48]{4,3,2,1,0:T(2,128)(2,1)} %bitcast.17, f32[1,48]{1,0:T(1,128)} %bitcast.18, f32[1]{0:T(128)S(6)} %copy.13.dc_ref, bf16[2,2,192,384]{3,2,1,0:T(8,128)(2,1)} %bitcast.13, ...), custom_call_target="tpu_custom_call" | custom-call | tf_op jit(solution)/shard_map/cascade/pallas_call | solution.py:500
  25.7 0.9 %reshape.3 = f32[48,1,2,2,192]{4,3,2,0,1:T(2,128)} reshape(f32[48,768]{1,0:T(8,128)S(1)} %cascade.1) | data formatting | bytes 294912 | tf_op jit(solution)/shard_map/reshape | solution.py:550

commit v3 on v2

--- a/solution.py
+++ b/solution.py
@@ -1,4 +1,5 @@
 import functools
+import math
 
 import numpy as np
 import jax
@@ -14,7 +15,7 @@
 SLAB = 32
 GRANT = 24 << 20
 TINY = float(np.finfo(np.float32).tiny)
-SPLITS = (3, 8, 10, 11)
+SPLITS = (7, 7, 11, 11)
 
 
 def tables(length):
@@ -109,11 +110,13 @@
                     barrier, inc=1, device_id=(up(d) // n_r, c + step, lax.rem(up(d), n_r)), device_id_type=MESH
                 )
     margin = rq + 2
+    padded[...] = jnp.zeros_like(padded)
     loads[0].wait()
     flat[...] = jnp.concatenate([image[:, s, p, :] for s in range(s_local) for p in range(2)], axis=1)
     for s in range(s_local):
         gat[s, c] = flat[:, s * width : (s + 1) * width].astype(BF16)
 
+    padded[margin : margin + rb, :, :nz] = image[...].reshape(rb, 2 * s_local, nz).astype(BF16)
     sides = jnp.minimum(c, 1) + jnp.minimum(n_c - 1 - c, 1)
     pl.semaphore_wait(barrier, chips + peers - 1 + peers * sides)
 
@@ -165,8 +168,6 @@
     near = range(1, chips)
     far = near[::-1]
 
-    padded[...] = jnp.zeros_like(padded)
-    padded[margin : margin + rb, :, :nz] = image[...].reshape(rb, 2 * s_local, nz).astype(BF16)
     for d in range(1, peers):
         when(active(up(d)), lambda: window(d).start())
     pl.when(c < n_c - 1)(lambda: edge_up().start())
@@ -187,6 +188,7 @@
 
     count = filters.shape[-1]
     slices = s_local * n_r
+    band = pen_send.shape[3]
     for load in loads[1:4]:
         load.wait()
     flat_filters = filters[...].astype(F32).reshape(-1, count).astype(BF16)
@@ -265,7 +267,10 @@
             high = jnp.where(lane > 0, high, 0.0)
             total = low + held[:, taps : 2 * taps] + high
             for read in range(n_r):
-                pen_send[echo, read] = total[:, read * 2 * s_local : (read + 1) * 2 * s_local].astype(BF16)
+                own = range(read * 2 * s_local, (read + 1) * 2 * s_local)
+                dense = jnp.concatenate([total[:, k, :nz] for k in own], axis=1)
+                for k in range(rq // band):
+                    pen_send[echo, read, k] = dense[k * band : (k + 1) * band]
         pen_recv[q] = pen_send[e, r]
 
     def penalty_out(d):
@@ -378,17 +383,17 @@
 
     turn()
     rows(0)
-    rows(1)
     relay(0, near)
     columns(0, core)
     complete(0)
     columns(0, 1 - core)
     fronts(0)
     middle()
+    backs(0, 0)
     relay(1, near)
-    backs(0, 0)
     backs(0, 1)
     columns(1, core)
+    rows(1)
     send_sums(0, 0)
     complete(1)
     columns(1, 1 - core)
@@ -412,8 +417,10 @@
                     pen_send.at[0, 0], pen_recv.at[src], p_send_sem.at[d], p_recv_sem.at[d], (e, c, r)
                 ).wait_recv(),
             )
-        held = pen_recv[...].astype(F32).reshape(rb, 2 * s_local, zp)
-        flat[...] = flat[...] - jnp.concatenate([held[:, k, :nz] for k in range(2 * s_local)], axis=1)
+        for at in range(n_q):
+            for k in range(rq // band):
+                row = at * rq + k * band
+                flat[row : row + band, :] = flat[row : row + band, :] - pen_recv[at, k]
 
     def hops(s):
         for d in range(1, chips):
@@ -462,6 +469,7 @@
     width = 2 * nz
     slices = s_local * n_r
     taps = 2 * slices
+    band = math.gcd(rq, 4)
     count = filters.shape[0]
 
     col_cos, col_sin = tables(nz)
@@ -519,8 +527,8 @@
             pltpu.VMEM((slices * count, zp), F32),
             pltpu.VMEM((n_e, n_r, rq + 4, 2 * s_local, zp), BF16),
             pltpu.VMEM((2, n_e, n_r, 2, 2 * s_local, zp), BF16),
-            pltpu.VMEM((n_e, n_r, rq, 2 * s_local, zp), BF16),
-            pltpu.VMEM((n_q, rq, 2 * s_local, zp), BF16),
+            pltpu.VMEM((n_e, n_r, rq // band, band, s_local * width), F32),
+            pltpu.VMEM((n_q, rq // band, band, s_local * width), F32),
             pltpu.VMEM((n_e, rq + 4, SLAB, zp), F32),
             pltpu.VMEM((n_e, (rq + 4) * SLAB, zp), BF16),
             pltpu.VMEM(k_view.shape, BF16),

time: 26.7 us -> 26 us (0.974)
  Pallas kernels: 25 us -> 24.3 us
    pallas_call x1, Pallas kernels: 25 us -> 24.3 us  [body(): pl.pallas_call(functools.partial(kernel, (n_e, n_c, n_r, n_q, rq, nz, ny)...]
where the time goes in v3:
time: 26 us; the launch traced here: 25.9 us
  Pallas kernels  24.3 us (93%)
  local copies, waits for them, and re-layouts  0.87 us (3%)
  between operations  0.66 us (3%)
    pallas_call x1, Pallas kernels, body(): pl.pallas_call(functools.partial(kernel, (n_e, n_c, n_r, n_q, rq, nz, ny)...  24.3 us
    reshape x1, local copies, waits for them, and re-layouts, body(): return updated.reshape(image.shape)  0.87 us

profile of v3, /device:TPU:0, one launch (start us, length us, event | category | flops | bytes accessed | tf_op | source)
XLA Modules:
  0.0 25.9 jit_solution(14776774347012490410)
XLA Ops:
  0.7 24.3 %cascade.1 = f32[48,768]{1,0:T(8,128)S(1)} custom-call(f32[48,2,2,192]{3,2,1,0:T(2,128)} %bitcast.16, bf16[4,96,54]{2,1,0:T(8,128)(2,1)} %constant.11.clone.spread_hbm, bf16[3,3,3,2,48]{4,3,2,1,0:T(2,128)(2,1)} %bitcast.17, f32[1,48]{1,0:T(1,128)} %bitcast.18, f32[1]{0:T(128)S(6)} %copy.13.dc_ref, bf16[2,2,192,384]{3,2,1,0:T(8,128)(2,1)} %bitcast.13, ...), custom_call_target="tpu_custom_call" | custom-call | tf_op jit(solution)/shard_map/cascade/pallas_call | solution.py:508
  25.0 0.9 %reshape.3 = f32[48,1,2,2,192]{4,3,2,0,1:T(2,128)} reshape(f32[48,768]{1,0:T(8,128)S(1)} %cascade.1) | data formatting | bytes 294912 | tf_op jit(solution)/shard_map/reshape | solution.py:558

commit v4 on v3

--- a/solution.py
+++ b/solution.py
@@ -168,11 +168,12 @@
     near = range(1, chips)
     far = near[::-1]
 
-    for d in range(1, peers):
-        when(active(up(d)), lambda: window(d).start())
     pl.when(c < n_c - 1)(lambda: edge_up().start())
     pl.when(c > 0)(lambda: edge_down().start())
     for s in range(s_local):
+        if s == s_local - 1:
+            for d in range(1, peers):
+                when(active(up(d)), lambda: window(d).start())
         targets(lambda d: gather(s, d).start(), near if s else far)
         gather(s, None).start()
 
@@ -329,8 +330,9 @@
         h = halves(j)
         sums = (part[s, h, :, core].astype(F32) + paired[s, h].astype(F32)).astype(BF16)
         for k in range(group):
-            to = h * group + k
-            rs_send[s, to] = sums[k]
+            rs_send[s, h * group + k] = sums[k]
+        for k in range(group):
+            to = h * group + jnp.where(h == 1, group - 1 - k, k)
             if j:
                 pl.when(to != chip)(lambda: scatter(s, to).start())
             else:

time: 26 us -> 26 us (level)
  no operation moved by 1% of the time
where the time goes in v4:
time: 26 us; the launch traced here: 25.9 us
  Pallas kernels  24.3 us (93%)
  local copies, waits for them, and re-layouts  0.87 us (3%)
  between operations  0.66 us (3%)
    pallas_call x1, Pallas kernels, body(): pl.pallas_call(functools.partial(kernel, (n_e, n_c, n_r, n_q, rq, nz, ny)...  24.3 us
    reshape x1, local copies, waits for them, and re-layouts, body(): return updated.reshape(image.shape)  0.87 us

profile of v4, /device:TPU:0, one launch (start us, length us, event | category | flops | bytes accessed | tf_op | source)
XLA Modules:
  0.0 25.9 jit_solution(4807807485371903060)
XLA Ops:
  0.7 24.3 %cascade.1 = f32[48,768]{1,0:T(8,128)S(1)} custom-call(f32[48,2,2,192]{3,2,1,0:T(2,128)} %bitcast.16, bf16[4,96,54]{2,1,0:T(8,128)(2,1)} %constant.11.clone.spread_hbm, bf16[3,3,3,2,48]{4,3,2,1,0:T(2,128)(2,1)} %bitcast.17, f32[1,48]{1,0:T(1,128)} %bitcast.18, f32[1]{0:T(128)S(6)} %copy.13.dc_ref, bf16[2,2,192,384]{3,2,1,0:T(8,128)(2,1)} %bitcast.13, ...), custom_call_target="tpu_custom_call" | custom-call | tf_op jit(solution)/shard_map/cascade/pallas_call | solution.py:510
  25.0 0.9 %reshape.3 = f32[48,1,2,2,192]{4,3,2,0,1:T(2,128)} reshape(f32[48,768]{1,0:T(8,128)S(1)} %cascade.1) | data formatting | bytes 294912 | tf_op jit(solution)/shard_map/reshape | solution.py:560

commit v5 on v4

--- a/solution.py
+++ b/solution.py
@@ -100,15 +100,16 @@
     for d in range(chips):
         to = lax.rem(c + 2 * d, n_c) if d else partner
         pl.semaphore_signal(barrier, inc=1, device_id=(e, to, r), device_id_type=MESH)
-    for d in range(peers):
-        if d:
-            pl.semaphore_signal(barrier, inc=1, device_id=(up(d) // n_r, c, lax.rem(up(d), n_r)), device_id_type=MESH)
-        for step, ok in ((1, c < n_c - 1), (-1, c > 0)):
-            @pl.when(ok)
-            def _():
-                pl.semaphore_signal(
-                    barrier, inc=1, device_id=(up(d) // n_r, c + step, lax.rem(up(d), n_r)), device_id_type=MESH
-                )
+    for d in range(1, peers):
+        pl.semaphore_signal(barrier, inc=1, device_id=(up(d) // n_r, c, lax.rem(up(d), n_r)), device_id_type=MESH)
+    last = n_q - 1
+
+    def greet(step):
+        for at in range(peers):
+            pl.semaphore_signal(barrier, inc=1, device_id=(at // n_r, c + step, at % n_r), device_id_type=MESH)
+
+    pl.when(jnp.logical_and(q == 0, c > 0))(lambda: greet(-1))
+    pl.when(jnp.logical_and(q == last, c < n_c - 1))(lambda: greet(1))
     margin = rq + 2
     padded[...] = jnp.zeros_like(padded)
     loads[0].wait()
@@ -118,7 +119,7 @@
 
     padded[margin : margin + rb, :, :nz] = image[...].reshape(rb, 2 * s_local, nz).astype(BF16)
     sides = jnp.minimum(c, 1) + jnp.minimum(n_c - 1 - c, 1)
-    pl.semaphore_wait(barrier, chips + peers - 1 + peers * sides)
+    pl.semaphore_wait(barrier, chips + peers - 1 + sides)
 
     def window(d):
         to = up(d)
@@ -126,7 +127,6 @@
             padded.at[pl.ds((1 + to) * rq, rq + 4)], ext.at[e, r], x_send_sem.at[d], x_recv_sem.at[d], (to // n_r, c, lax.rem(to, n_r))
         )
 
-    last = n_q - 1
     def edge_up():
         return remote(
             padded.at[pl.ds(margin + rb - 2, 2)], edge.at[0, e, r], e_send_sem.at[0], e_recv_sem.at[0, q], (0, c + 1, 0)

time: 26 us -> 25.9 us (level)
  no operation moved by 1% of the time
where the time goes in v5:
time: 25.9 us; the launch traced here: 25.7 us
  Pallas kernels  24.2 us (93%)
  local copies, waits for them, and re-layouts  0.87 us (3%)
  between operations  0.66 us (3%)
    pallas_call x1, Pallas kernels, body(): pl.pallas_call(functools.partial(kernel, (n_e, n_c, n_r, n_q, rq, nz, ny)...  24.2 us
    reshape x1, local copies, waits for them, and re-layouts, body(): return updated.reshape(image.shape)  0.87 us

profile of v5, /device:TPU:0, one launch (start us, length us, event | category | flops | bytes accessed | tf_op | source)
XLA Modules:
  0.0 25.7 jit_solution(17594443065010093172)
XLA Ops:
  0.7 24.2 %cascade.1 = f32[48,768]{1,0:T(8,128)S(1)} custom-call(f32[48,2,2,192]{3,2,1,0:T(2,128)} %bitcast.16, bf16[4,96,54]{2,1,0:T(8,128)(2,1)} %constant.11.clone.spread_hbm, bf16[3,3,3,2,48]{4,3,2,1,0:T(2,128)(2,1)} %bitcast.17, f32[1,48]{1,0:T(1,128)} %bitcast.18, f32[1]{0:T(128)S(6)} %copy.13.dc_ref, bf16[2,2,192,384]{3,2,1,0:T(8,128)(2,1)} %bitcast.13, ...), custom_call_target="tpu_custom_call" | custom-call | tf_op jit(solution)/shard_map/cascade/pallas_call | solution.py:510
  24.9 0.9 %reshape.3 = f32[48,1,2,2,192]{4,3,2,0,1:T(2,128)} reshape(f32[48,768]{1,0:T(8,128)S(1)} %cascade.1) | data formatting | bytes 294912 | tf_op jit(solution)/shard_map/reshape | solution.py:560
